TPU v7x, 32 devices: a whole 2x2x4 slice. The times are simulated.
32 devices in a mesh: tm: 2 (over x), grid: 16 (over z, y, core).
Axes of the slice: x: 2, y: 2, z: 4, core: 2. Of those that a mesh axis runs over, the one named last changes fastest.
Arguments:
- occupied_green: bfloat16 [2, 1024, 1024], P('tm', 'grid'), may hold values from -0.005859375 to 0.005859375
- empty_green: bfloat16 [2, 1024, 1024], P('tm', 'grid'), may hold values from -0.005859375 to 0.005859375
- basis: bfloat16 [12288, 1024], P('grid'), may hold values from -8 to 8
- time_weights: float32 [2, 2], replicated, may hold values from 0.25 to 1
Outputs:
- polarizability: float32 [2, 1024, 1024], P('tm', 'grid')
All inputs are finite; a program needn't handle non-finite values.
Results may differ from a plain program's by a relative error of at most 0.0012.
Values may be sent and summed in bfloat16 or wider, within the bound.
A program may use at most 128 MiB of HBM per device.

v0:
```python
import jax
import jax.numpy as jnp
from jax import lax
from jax.sharding import PartitionSpec as P

NR = 12288
NB = 1024


def weigh_times(time_weights, block_list, scale_factor):
    time_count = len(block_list)
    group_index = lax.axis_index("tm")
    weights_local = lax.dynamic_slice_in_dim(time_weights, group_index * time_count, time_count, 1)
    accum = weights_local[:, 0, None, None] * block_list[0][None]
    return scale_factor * accum


def step_size(piece_rows):
    return max((divisor for divisor in range(1, 2049) if piece_rows % divisor == 0))


def shards(occupied_green, empty_green, basis, time_weights):
    stacked = jnp.stack([occupied_green, empty_green])
    time_count = occupied_green.shape[0]
    coef_block = occupied_green.shape[1]
    row_total = basis.shape[0]
    scale_factor = 1.0 / NR

    def make_accumulate(combined_rows):

        def accumulate(running, basis_piece, first_row):
            piece_rows = basis_piece.shape[0]
            step_rows = step_size(piece_rows)

            def one_step(step_index, inner):
                basis_subpart = lax.dynamic_slice_in_dim(
                    basis_piece, step_index * step_rows, step_rows, 0
                )
                real_pair = jnp.einsum(
                    "qoa,ba->qob", combined_rows, basis_subpart, preferred_element_type=jnp.float32
                )
                product = (real_pair[0] * real_pair[1]).astype(jnp.bfloat16)
                return inner + jnp.dot(product, basis_subpart, preferred_element_type=jnp.float32)

            return lax.fori_loop(0, piece_rows // step_rows, one_step, running)

        return accumulate

    initial = jnp.zeros((time_count * row_total, NB), jnp.float32)
    projected = jnp.einsum(
        "sl,ftkl->ftsk",
        basis,
        lax.all_gather(stacked, "grid", axis=2, tiled=True),
        preferred_element_type=jnp.float32,
    ).astype(jnp.bfloat16)
    combined_rows = projected.reshape(2, time_count * row_total, NB)
    accumulate = make_accumulate(combined_rows)
    summed = accumulate(initial, lax.all_gather(basis, "grid", axis=0, tiled=True), jnp.int32(0))
    back_half = summed.astype(jnp.bfloat16).reshape(time_count, row_total, NB)
    coef_rows = lax.psum_scatter(
        jnp.einsum("tsk,sl->ktl", back_half, basis, preferred_element_type=jnp.float32).reshape(
            lax.axis_size("grid") * coef_block, time_count * NB
        ),
        "grid",
        scatter_dimension=0,
        tiled=True,
    ).reshape(coef_block, time_count, NB)
    block_list = [coef_rows[:, 0]]
    result = lax.psum_scatter(
        weigh_times(time_weights, block_list, scale_factor), "tm", scatter_dimension=0, tiled=True
    )
    return result


def solution(mesh):
    in_specs = (P("tm", "grid", None), P("tm", "grid", None), P("grid", None), P())
    out_specs = P("tm", "grid", None)
    return jax.shard_map(shards, mesh=mesh, in_specs=in_specs, out_specs=out_specs, check_vma=False)
```

profile of v0, /device:TPU:0, one launch (start us, length us, event | category | flops | bytes accessed | tf_op | source)
XLA Modules:
  0.0 431.6 jit_solution(16188916720244867342)
XLA Ops:
  6.5 0.0 copy-start
  6.5 0.0 all-gather.5.cloned.1.call-start
  6.5 1.7 pad_maximum_fusion
  8.2 0.0 all-gather.5.cloned.1.call-update
  8.3 0.0 all-gather.3.cloned.1.call-start
  8.3 0.7 all-gather.3.cloned.1.call-update
  9.0 0.0 reduce-scatter.3.cloned.1.call-start
  9.1 53.6 %all-gather.5.cloned.1.call-done = bf16[2,1,1024,1024]{3,2,0,1:T(8,128)(2,1)} async-done(((bf16[2,1,64,1024]{3,2,0,1:T(8,128)(2,1)}), bf16[2,1,1024,1024]{3,2,0,1:T(8,128)(2,1)}) %all-gather.5.cloned.1.call-update) | async-done | bytes 4194320 | tf_op jit(solution)/shard_map/all_gather | solution.py:53
  62.7 7.9 %convert_bitcast_fusion = bf16[2,768,1024]{1,2,0:T(8,128)(2,1)} fusion(bf16[2,1,1024,1024]{3,2,0,1:T(8,128)(2,1)} %all-gather.5.cloned.1.call-done, bf16[768,1024]{1,0:T(8,128)(2,1)} %param.8), kind=kOutput, calls=%fused_computation.13 | convolution fusion | flops 3222798336 | bytes 8912896 | tf_op jit(solution)/shard_map/sl,ftkl->ftsk/dot_general | solution.py:50
  70.5 3.2 copy.5
  73.8 117.6 %all-gather.3.cloned.1.call-done = bf16[12288,1024]{1,0:T(8,128)(2,1)} async-done(((bf16[768,1024]{1,0:T(8,128)(2,1)}), bf16[12288,1024]{1,0:T(8,128)(2,1)}) %all-gather.3.cloned.1.call-update) | async-done | bytes 25165840 | tf_op jit(solution)/shard_map/all_gather | solution.py:58
  191.3 138.8 %while.14 = (s32[]{:T(128)}, f32[768,1024]{1,0:T(8,128)}, bf16[12288,1024]{1,0:T(8,128)(2,1)}, bf16[2,768,1024]{2,1,0:T(8,128)(2,1)S(1)}, s32[]{:T(128)}, /*index=5*/s32[]{:T(128)}, s32[]{:T(128)}, s32[]{:T(128)}) while((s32[]{:T(128)}, f32[768,1024]{1,0:T(8,128)}, bf16[12288,1024]{1,0:T(8,128)(2,1)}, ...), condition=%wide.region_1.0_spmd.clone, body=%wide.region_0.0_spmd.clone.sunk | while | flops 9668395008 | bytes 42991772 | solution.py:45
  191.4 11.5 %convolution_bitcast_fusion.2 = f32[2,768,2048]{1,2,0:T(8,128)} fusion(bf16[2,768,1024]{2,1,0:T(8,128)(2,1)S(1)} %get-tuple-element.156, bf16[12288,1024]{1,0:T(8,128)(2,1)} %get-tuple-element.155, s32[]{:T(128)S(6)} %select_n.13), kind=kOutput, calls=%fused_computation.2.clone.1 | convolution fusion | flops 6442450944 | bytes 19922948 | tf_op jit(solution)/shard_map/while/body/eval_jaxpr/qoa,ba->qob/dot_general | solution.py:39
  202.9 10.9 %select_add_fusion.2 = f32[768,1024]{1,0:T(8,128)} fusion(f32[768,1024]{1,0:T(8,128)} %get-tuple-element.146, bf16[12288,1024]{1,0:T(8,128)(2,1)} %get-tuple-element.155, s32[]{:T(128)S(6)} %select_n.13, f32[2,768,2048]{1,2,0:T(8,128)} %convolution_bitcast_fusion.2, pred[]{:T(512)S(6)} %compare.3), kind=kOutput, calls=%fused_computation.8.clone.1 | convolution fusion | flops 3225944064 | bytes 23068676 | tf_op jit(solution)/shard_map/while/body/eval_jaxpr/dot_general | solution.py:43
  213.7 11.5 %convolution_bitcast_fusion.2 = f32[2,768,2048]{1,2,0:T(8,128)} fusion(bf16[2,768,1024]{2,1,0:T(8,128)(2,1)S(1)} %get-tuple-element.156, bf16[12288,1024]{1,0:T(8,128)(2,1)} %get-tuple-element.155, s32[]{:T(128)S(6)} %select_n.13), kind=kOutput, calls=%fused_computation.2.clone.1 | convolution fusion | flops 6442450944 | bytes 19922948 | tf_op jit(solution)/shard_map/while/body/eval_jaxpr/qoa,ba->qob/dot_general | solution.py:39
  225.2 11.8 %select_add_fusion.2 = f32[768,1024]{1,0:T(8,128)} fusion(f32[768,1024]{1,0:T(8,128)} %get-tuple-element.146, bf16[12288,1024]{1,0:T(8,128)(2,1)} %get-tuple-element.155, s32[]{:T(128)S(6)} %select_n.13, f32[2,768,2048]{1,2,0:T(8,128)} %convolution_bitcast_fusion.2, pred[]{:T(512)S(6)} %compare.3), kind=kOutput, calls=%fused_computation.8.clone.1 | convolution fusion | flops 3225944064 | bytes 23068676 | tf_op jit(solution)/shard_map/while/body/eval_jaxpr/dot_general | solution.py:43
  237.0 11.5 %convolution_bitcast_fusion.2 = f32[2,768,2048]{1,2,0:T(8,128)} fusion(bf16[2,768,1024]{2,1,0:T(8,128)(2,1)S(1)} %get-tuple-element.156, bf16[12288,1024]{1,0:T(8,128)(2,1)} %get-tuple-element.155, s32[]{:T(128)S(6)} %select_n.13), kind=kOutput, calls=%fused_computation.2.clone.1 | convolution fusion | flops 6442450944 | bytes 19922948 | tf_op jit(solution)/shard_map/while/body/eval_jaxpr/qoa,ba->qob/dot_general | solution.py:39
  248.5 11.8 %select_add_fusion.2 = f32[768,1024]{1,0:T(8,128)} fusion(f32[768,1024]{1,0:T(8,128)} %get-tuple-element.146, bf16[12288,1024]{1,0:T(8,128)(2,1)} %get-tuple-element.155, s32[]{:T(128)S(6)} %select_n.13, f32[2,768,2048]{1,2,0:T(8,128)} %convolution_bitcast_fusion.2, pred[]{:T(512)S(6)} %compare.3), kind=kOutput, calls=%fused_computation.8.clone.1 | convolution fusion | flops 3225944064 | bytes 23068676 | tf_op jit(solution)/shard_map/while/body/eval_jaxpr/dot_general | solution.py:43
  260.3 11.5 %convolution_bitcast_fusion.2 = f32[2,768,2048]{1,2,0:T(8,128)} fusion(bf16[2,768,1024]{2,1,0:T(8,128)(2,1)S(1)} %get-tuple-element.156, bf16[12288,1024]{1,0:T(8,128)(2,1)} %get-tuple-element.155, s32[]{:T(128)S(6)} %select_n.13), kind=kOutput, calls=%fused_computation.2.clone.1 | convolution fusion | flops 6442450944 | bytes 19922948 | tf_op jit(solution)/shard_map/while/body/eval_jaxpr/qoa,ba->qob/dot_general | solution.py:39
  271.8 11.8 %select_add_fusion.2 = f32[768,1024]{1,0:T(8,128)} fusion(f32[768,1024]{1,0:T(8,128)} %get-tuple-element.146, bf16[12288,1024]{1,0:T(8,128)(2,1)} %get-tuple-element.155, s32[]{:T(128)S(6)} %select_n.13, f32[2,768,2048]{1,2,0:T(8,128)} %convolution_bitcast_fusion.2, pred[]{:T(512)S(6)} %compare.3), kind=kOutput, calls=%fused_computation.8.clone.1 | convolution fusion | flops 3225944064 | bytes 23068676 | tf_op jit(solution)/shard_map/while/body/eval_jaxpr/dot_general | solution.py:43
  283.6 11.5 %convolution_bitcast_fusion.2 = f32[2,768,2048]{1,2,0:T(8,128)} fusion(bf16[2,768,1024]{2,1,0:T(8,128)(2,1)S(1)} %get-tuple-element.156, bf16[12288,1024]{1,0:T(8,128)(2,1)} %get-tuple-element.155, s32[]{:T(128)S(6)} %select_n.13), kind=kOutput, calls=%fused_computation.2.clone.1 | convolution fusion | flops 6442450944 | bytes 19922948 | tf_op jit(solution)/shard_map/while/body/eval_jaxpr/qoa,ba->qob/dot_general | solution.py:39
  295.1 11.8 %select_add_fusion.2 = f32[768,1024]{1,0:T(8,128)} fusion(f32[768,1024]{1,0:T(8,128)} %get-tuple-element.146, bf16[12288,1024]{1,0:T(8,128)(2,1)} %get-tuple-element.155, s32[]{:T(128)S(6)} %select_n.13, f32[2,768,2048]{1,2,0:T(8,128)} %convolution_bitcast_fusion.2, pred[]{:T(512)S(6)} %compare.3), kind=kOutput, calls=%fused_computation.8.clone.1 | convolution fusion | flops 3225944064 | bytes 23068676 | tf_op jit(solution)/shard_map/while/body/eval_jaxpr/dot_general | solution.py:43
  306.9 11.5 %convolution_bitcast_fusion.2 = f32[2,768,2048]{1,2,0:T(8,128)} fusion(bf16[2,768,1024]{2,1,0:T(8,128)(2,1)S(1)} %get-tuple-element.156, bf16[12288,1024]{1,0:T(8,128)(2,1)} %get-tuple-element.155, s32[]{:T(128)S(6)} %select_n.13), kind=kOutput, calls=%fused_computation.2.clone.1 | convolution fusion | flops 6442450944 | bytes 19922948 | tf_op jit(solution)/shard_map/while/body/eval_jaxpr/qoa,ba->qob/dot_general | solution.py:39
  318.4 11.8 %select_add_fusion.2 = f32[768,1024]{1,0:T(8,128)} fusion(f32[768,1024]{1,0:T(8,128)} %get-tuple-element.146, bf16[12288,1024]{1,0:T(8,128)(2,1)} %get-tuple-element.155, s32[]{:T(128)S(6)} %select_n.13, f32[2,768,2048]{1,2,0:T(8,128)} %convolution_bitcast_fusion.2, pred[]{:T(512)S(6)} %compare.3), kind=kOutput, calls=%fused_computation.8.clone.1 | convolution fusion | flops 3225944064 | bytes 23068676 | tf_op jit(solution)/shard_map/while/body/eval_jaxpr/dot_general | solution.py:43
  330.2 6.1 %fusion.18 = f32[1024,1024]{1,0:T(8,128)} fusion(bf16[768,1024]{1,0:T(8,128)(2,1)} %param.8, f32[768,1024]{1,0:T(8,128)} %get-tuple-element.84), kind=kOutput, calls=%fused_computation.15 | convolution fusion | flops 1611399168 | bytes 8912896 | tf_op jit(solution)/shard_map/tsk,sl->ktl/dot_general | solution.py:61
  336.3 0.0 reduce-scatter.3.cloned.1.call-update
  336.3 0.0 reduce-scatter.5.cloned.1.call-start
  336.4 0.0 copy-done
  336.4 0.2 dynamic-slice_reduce_fusion
  336.6 72.7 %reduce-scatter.3.cloned.1.call-done = f32[64,1024]{1,0:T(8,128)} async-done(((f32[1024,1024]{1,0:T(8,128)}), f32[64,1024]{1,0:T(8,128)}) %reduce-scatter.3.cloned.1.call-update) | async-done | bytes 262160 | tf_op jit(solution)/shard_map/reduce_scatter | solution.py:60
  409.2 1.9 multiply_multiply_fusion
  411.1 0.0 reduce-scatter.5.cloned.1.call-update
  411.1 13.9 %reduce-scatter.5.cloned.1.call-done = f32[1,64,1024]{2,1,0:T(8,128)} async-done(((f32[2,64,1024]{2,1,0:T(8,128)}), f32[1,64,1024]{2,1,0:T(8,128)}) %reduce-scatter.5.cloned.1.call-update) | async-done | bytes 262160 | tf_op jit(solution)/shard_map/reduce_scatter | solution.py:69
  (1 shorter events, 0.0 us)
Async XLA Ops:
  6.5 329.8 %copy-start = (f32[2,2]{1,0:T(2,128)S(1)}, f32[2,2]{1,0:T(2,128)}, u32[]{:S(2)}) copy-start(f32[2,2]{1,0:T(2,128)} %param.9) | copy-start | bytes 52
  6.5 56.1 %all-gather.5.cloned.1.call-start = ((), (), s32[]{:S(2)}) async-start(), calls=%async_computation.3 | async-start | bytes 4456448 | tf_op jit(solution)/shard_map/all_gather | solution.py:53
  8.3 183.1 %all-gather.3.cloned.1.call-start = ((), (), s32[]{:S(2)}) async-start(), calls=%async_computation.2 | async-start | bytes 26738688 | tf_op jit(solution)/shard_map/all_gather | solution.py:58
  9.0 400.2 %reduce-scatter.3.cloned.1.call-start = ((), (), s32[]{:S(2)}) async-start(), calls=%async_computation.4 | async-start | bytes 4456448 | tf_op jit(solution)/shard_map/reduce_scatter | solution.py:60
  336.3 88.8 %reduce-scatter.5.cloned.1.call-start = ((), (), s32[]{:S(2)}) async-start(), calls=%async_computation.5 | async-start | bytes 786432 | tf_op jit(solution)/shard_map/reduce_scatter | solution.py:69
Sparse Core Ops, SparseCore 0:
  9.5 53.1 all-gather.4
  64.3 127.0 all-gather.2
  336.4 72.7 reduce-scatter.2
  411.3 13.6 reduce-scatter.4
where the time goes:
time: 432 us
  waiting for transfers between devices  259 us (60%)
  matrix products  153 us (35%)
  between operations  13.2 us (3%)
    all_gather x1, waiting for transfers between devices, shards(): lax.all_gather(basis, 'grid', axis=0, tiled=True)  118 us
    reduce_scatter x1, waiting for transfers between devices, shards(): lax.psum_scatter(jnp.einsum('tsk,sl->ktl', back_half, basis, preferred_el...  72.7 us
    dot_general x6, matrix products, one_step(): jnp.dot(product, basis_subpart, preferred_element_type=jnp.float32)  69.8 us
    dot_general x6, matrix products, one_step(): jnp.einsum('qoa,ba->qob', combined_rows, basis_subpart, preferred_element...  69 us
    all_gather x1, waiting for transfers between devices, shards(): lax.all_gather(stacked, 'grid', axis=2, tiled=True)  53.6 us
    reduce_scatter x1, waiting for transfers between devices, shards(): lax.psum_scatter(weigh_times(time_weights, block_list, scale_factor), 'tm...  13.9 us
  transfers between devices with their start and end apart: 4, of which 4 were waited for; matrix products, arithmetic and copies ran while one was open for 3% of the time, Pallas kernels for 0%

commit v1 on v0

--- a/solution.py
+++ b/solution.py
@@ -5,6 +5,18 @@
 
 NR = 12288
 NB = 1024
+
+
+def gather_by_bits(shard, axis, dim):
+    ways, here = (lax.axis_size(axis), lax.axis_index(axis))
+    grown, reach = (shard, 1)
+    while reach < ways:
+        theirs = lax.ppermute(grown, axis, [(d, d ^ reach) for d in range(ways)])
+        mine_first = jnp.concatenate([grown, theirs], axis=dim)
+        theirs_first = jnp.concatenate([theirs, grown], axis=dim)
+        grown = jnp.where(here & reach == 0, mine_first, theirs_first)
+        reach = 2 * reach
+    return grown
 
 
 def weigh_times(time_weights, block_list, scale_factor):
@@ -50,7 +62,7 @@
     projected = jnp.einsum(
         "sl,ftkl->ftsk",
         basis,
-        lax.all_gather(stacked, "grid", axis=2, tiled=True),
+        gather_by_bits(stacked, "grid", 2),
         preferred_element_type=jnp.float32,
     ).astype(jnp.bfloat16)
     combined_rows = projected.reshape(2, time_count * row_total, NB)

time: 432 us -> 439 us (1.016)
  matrix products: 153 us -> 100 us
  waiting for transfers between devices: 259 us -> 296 us
  local copies, waits for them, and re-layouts: 3.4 us -> 13.7 us
  other arithmetic: 3.57 us -> 9.73 us
  starting transfers between devices: 0.12 us -> 5.87 us
    ppermute x0 -> x4, waiting for transfers between devices: none -> 201 us  [gather_by_bits(): theirs = lax.ppermute(grown, axis, [(d, d ^ reach) for d in range(ways)])]
    all_gather x1, waiting for transfers between devices: 118 us -> 0.02 us  [shards(): lax.all_gather(basis, 'grid', axis=0, tiled=True)]
    all_gather x1 -> x0, waiting for transfers between devices: 53.6 us -> none  [shards(): lax.all_gather(stacked, 'grid', axis=2, tiled=True)]
    dot_general x6, matrix products: 69.8 us -> 33.9 us  [one_step(): jnp.dot(product, basis_subpart, preferred_element_type=jnp.float32)]
    dot_general x6, matrix products: 69 us -> 52.4 us  [one_step(): jnp.einsum('qoa,ba->qob', combined_rows, basis_subpart, preferred_element...]
    while x0 -> x24, local copies, waits for them, and re-layouts: none -> 10.3 us
    reduce_scatter x1, waiting for transfers between devices: 72.7 us -> 79.8 us  [shards(): lax.psum_scatter(jnp.einsum('tsk,sl->ktl', back_half, basis, preferred_el...]
    select_n x0 -> x6, other arithmetic: none -> 6.86 us  [gather_by_bits(): grown = jnp.where(here & reach == 0, mine_first, theirs_first)]
  transfers between devices with their start and end apart: 4 -> 7, of which waited for: 4 -> 6; matrix products, arithmetic and copies ran while one was open for 3% -> 4% of each run, Pallas kernels for 0% -> 0%
where the time goes in v1:
time: 439 us
  waiting for transfers between devices  296 us (67%)
  matrix products  100 us (23%)
  local copies, waits for them, and re-layouts  13.7 us (3%)
  between operations  13.2 us (3%)
  other arithmetic  9.73 us (2%)
  starting transfers between devices  5.87 us (1%)
    ppermute x4, waiting for transfers between devices, gather_by_bits(): theirs = lax.ppermute(grown, axis, [(d, d ^ reach) for d in range(ways)])  201 us
    reduce_scatter x1, waiting for transfers between devices, shards(): lax.psum_scatter(jnp.einsum('tsk,sl->ktl', back_half, basis, preferred_el...  79.8 us
    dot_general x6, matrix products, one_step(): jnp.einsum('qoa,ba->qob', combined_rows, basis_subpart, preferred_element...  52.4 us
    dot_general x6, matrix products, one_step(): jnp.dot(product, basis_subpart, preferred_element_type=jnp.float32)  33.9 us
    reduce_scatter x1, waiting for transfers between devices, shards(): lax.psum_scatter(weigh_times(time_weights, block_list, scale_factor), 'tm...  14 us
    while x24, local copies, waits for them, and re-layouts  10.3 us
  transfers between devices with their start and end apart: 7, of which 6 were waited for; matrix products, arithmetic and copies ran while one was open for 4% of the time, Pallas kernels for 0%

profile of v1, /device:TPU:0, one launch (start us, length us, event | category | flops | bytes accessed | tf_op | source)
XLA Modules:
  0.0 438.8 jit_solution(10422748852394842231)
XLA Ops:
  6.5 0.0 copy-start
  6.5 0.0 all-gather.2.cloned.1.call-start
  6.5 0.7 all-gather.2.cloned.1.call-update
  7.3 0.0 reduce-scatter.3.cloned.1.call-start
  7.3 1.0 fusion.27
  8.3 0.6 collective-permute-start
  8.9 1.2 collective-permute-done
  10.0 1.2 fusion.25
  11.2 2.9 collective-permute-start.1
  14.1 0.1 maximum_select_fusion.6
  14.3 19.8 %collective-permute-done.1 = bf16[2,1,128,1024]{3,2,1,0:T(8,128)(2,1)S(1)} collective-permute-done((bf16[2,1,128,1024]{3,2,1,0:T(8,128)(2,1)S(1)}, bf16[2,1,128,1024]{3,2,1,0:T(8,128)(2,1)S(1)}, u32[]{:S(2)}, u32[]{:S(2)}) %collective-permute-start.1) | collective-permute-done | bytes 524320 | tf_op jit(solution)/shard_map/ppermute | solution.py:14
  34.0 1.5 fusion.24
  35.6 0.0 collective-permute-start.2
  35.6 0.5 maximum_select_fusion.5
  36.1 47.1 %collective-permute-done.2 = bf16[2,1,256,1024]{3,2,1,0:T(8,128)(2,1)S(1)} collective-permute-done((bf16[2,1,256,1024]{3,2,1,0:T(8,128)(2,1)}, bf16[2,1,256,1024]{3,2,1,0:T(8,128)(2,1)S(1)}, u32[]{:S(2)}, u32[]{:S(2)}) %collective-permute-start.2) | collective-permute-done | bytes 1048608 | tf_op jit(solution)/shard_map/ppermute | solution.py:14
  83.2 2.5 fusion.20
  85.8 2.3 collective-permute-start.3
  88.1 1.0 maximum_select_fusion.4
  89.1 133.3 %collective-permute-done.3 = bf16[2,1,512,1024]{3,2,1,0:T(8,128)(2,1)} collective-permute-done((bf16[2,1,512,1024]{3,2,1,0:T(8,128)(2,1)}, bf16[2,1,512,1024]{3,2,1,0:T(8,128)(2,1)}, u32[]{:S(2)}, u32[]{:S(2)}) %collective-permute-start.3) | collective-permute-done | bytes 2097184 | tf_op jit(solution)/shard_map/ppermute | solution.py:14
  222.3 0.0 copy-done.1
  222.3 7.8 %convert_bitcast_fusion = bf16[2,768,1024]{1,2,0:T(8,128)(2,1)} fusion(bf16[2,512,1024]{2,1,0:T(8,128)(2,1)} %bitcast.18, bf16[2,512,1024]{2,1,0:T(8,128)(2,1)S(1)} %maximum_select_fusion.4, pred[]{:T(512)S(6)} %eq.12, bf16[768,1024]{1,0:T(8,128)(2,1)S(1)} %copy-done.1), kind=kOutput, calls=%fused_computation.19 | convolution fusion | flops 3241672704 | bytes 8912897 | tf_op jit(solution)/shard_map/sl,ftkl->ftsk/dot_general | solution.py:62
  230.1 3.2 copy.15
  233.3 0.0 all-gather.2.cloned.1.call-done
  233.3 96.8 %while.14 = (s32[]{:T(128)}, f32[768,1024]{1,0:T(8,128)}, bf16[12288,1024]{1,0:T(8,128)(2,1)}, bf16[2,768,1024]{2,1,0:T(8,128)(2,1)S(1)}, s32[]{:T(128)}, /*index=5*/s32[]{:T(128)}, s32[]{:T(128)}, s32[]{:T(128)}) while((s32[]{:T(128)}, f32[768,1024]{1,0:T(8,128)}, bf16[12288,1024]{1,0:T(8,128)(2,1)}, ...), condition=%wide.region_1.2_spmd.clone, body=%wide.region_0.1_spmd.clone.sunk | while | flops 9668395008 | bytes 68157656 | solution.py:57
  233.4 0.0 copy-start.2
  233.4 8.7 %convolution_bitcast_fusion.2 = f32[2,768,2048]{1,2,0:T(8,128)S(1)} fusion(bf16[2,768,1024]{2,1,0:T(8,128)(2,1)S(1)} %get-tuple-element.158, bf16[12288,1024]{1,0:T(8,128)(2,1)} %get-tuple-element.157, s32[]{:T(128)S(6)} %select_n.144), kind=kOutput, calls=%fused_computation.2.clone.1 | convolution fusion | flops 6442450944 | bytes 19922948 | tf_op jit(solution)/shard_map/while/body/eval_jaxpr/qoa,ba->qob/dot_general | solution.py:51
  242.1 0.0 copy-done.2
  242.1 5.7 %select_add_fusion.2 = f32[768,1024]{1,0:T(8,128)S(1)} fusion(f32[768,1024]{1,0:T(8,128)S(1)} %copy-done.2, bf16[12288,1024]{1,0:T(8,128)(2,1)} %get-tuple-element.157, s32[]{:T(128)S(6)} %select_n.144, f32[2,768,2048]{1,2,0:T(8,128)S(1)} %convolution_bitcast_fusion.2, pred[]{:T(512)S(6)} %compare.3), kind=kOutput, calls=%fused_computation.8.clone.1 | convolution fusion | flops 3225944064 | bytes 23068676 | tf_op jit(solution)/shard_map/while/body/eval_jaxpr/dot_general | solution.py:55
  247.8 0.0 copy-start.3
  247.8 1.7 copy-done.3
  249.5 8.7 %convolution_bitcast_fusion.2 = f32[2,768,2048]{1,2,0:T(8,128)S(1)} fusion(bf16[2,768,1024]{2,1,0:T(8,128)(2,1)S(1)} %get-tuple-element.158, bf16[12288,1024]{1,0:T(8,128)(2,1)} %get-tuple-element.157, s32[]{:T(128)S(6)} %select_n.144), kind=kOutput, calls=%fused_computation.2.clone.1 | convolution fusion | flops 6442450944 | bytes 19922948 | tf_op jit(solution)/shard_map/while/body/eval_jaxpr/qoa,ba->qob/dot_general | solution.py:51
  258.2 0.0 copy-done.2
  258.3 5.7 %select_add_fusion.2 = f32[768,1024]{1,0:T(8,128)S(1)} fusion(f32[768,1024]{1,0:T(8,128)S(1)} %copy-done.2, bf16[12288,1024]{1,0:T(8,128)(2,1)} %get-tuple-element.157, s32[]{:T(128)S(6)} %select_n.144, f32[2,768,2048]{1,2,0:T(8,128)S(1)} %convolution_bitcast_fusion.2, pred[]{:T(512)S(6)} %compare.3), kind=kOutput, calls=%fused_computation.8.clone.1 | convolution fusion | flops 3225944064 | bytes 23068676 | tf_op jit(solution)/shard_map/while/body/eval_jaxpr/dot_general | solution.py:55
  263.9 0.0 copy-start.3
  263.9 1.7 copy-done.3
  265.6 8.7 %convolution_bitcast_fusion.2 = f32[2,768,2048]{1,2,0:T(8,128)S(1)} fusion(bf16[2,768,1024]{2,1,0:T(8,128)(2,1)S(1)} %get-tuple-element.158, bf16[12288,1024]{1,0:T(8,128)(2,1)} %get-tuple-element.157, s32[]{:T(128)S(6)} %select_n.144), kind=kOutput, calls=%fused_computation.2.clone.1 | convolution fusion | flops 6442450944 | bytes 19922948 | tf_op jit(solution)/shard_map/while/body/eval_jaxpr/qoa,ba->qob/dot_general | solution.py:51
  274.4 0.0 copy-done.2
  274.4 5.7 %select_add_fusion.2 = f32[768,1024]{1,0:T(8,128)S(1)} fusion(f32[768,1024]{1,0:T(8,128)S(1)} %copy-done.2, bf16[12288,1024]{1,0:T(8,128)(2,1)} %get-tuple-element.157, s32[]{:T(128)S(6)} %select_n.144, f32[2,768,2048]{1,2,0:T(8,128)S(1)} %convolution_bitcast_fusion.2, pred[]{:T(512)S(6)} %compare.3), kind=kOutput, calls=%fused_computation.8.clone.1 | convolution fusion | flops 3225944064 | bytes 23068676 | tf_op jit(solution)/shard_map/while/body/eval_jaxpr/dot_general | solution.py:55
  280.0 0.0 copy-start.3
  280.1 1.7 copy-done.3
  281.8 8.7 %convolution_bitcast_fusion.2 = f32[2,768,2048]{1,2,0:T(8,128)S(1)} fusion(bf16[2,768,1024]{2,1,0:T(8,128)(2,1)S(1)} %get-tuple-element.158, bf16[12288,1024]{1,0:T(8,128)(2,1)} %get-tuple-element.157, s32[]{:T(128)S(6)} %select_n.144), kind=kOutput, calls=%fused_computation.2.clone.1 | convolution fusion | flops 6442450944 | bytes 19922948 | tf_op jit(solution)/shard_map/while/body/eval_jaxpr/qoa,ba->qob/dot_general | solution.py:51
  290.5 0.0 copy-done.2
  290.5 5.7 %select_add_fusion.2 = f32[768,1024]{1,0:T(8,128)S(1)} fusion(f32[768,1024]{1,0:T(8,128)S(1)} %copy-done.2, bf16[12288,1024]{1,0:T(8,128)(2,1)} %get-tuple-element.157, s32[]{:T(128)S(6)} %select_n.144, f32[2,768,2048]{1,2,0:T(8,128)S(1)} %convolution_bitcast_fusion.2, pred[]{:T(512)S(6)} %compare.3), kind=kOutput, calls=%fused_computation.8.clone.1 | convolution fusion | flops 3225944064 | bytes 23068676 | tf_op jit(solution)/shard_map/while/body/eval_jaxpr/dot_general | solution.py:55
  296.2 0.0 copy-start.3
  296.2 1.7 copy-done.3
  297.9 8.7 %convolution_bitcast_fusion.2 = f32[2,768,2048]{1,2,0:T(8,128)S(1)} fusion(bf16[2,768,1024]{2,1,0:T(8,128)(2,1)S(1)} %get-tuple-element.158, bf16[12288,1024]{1,0:T(8,128)(2,1)} %get-tuple-element.157, s32[]{:T(128)S(6)} %select_n.144), kind=kOutput, calls=%fused_computation.2.clone.1 | convolution fusion | flops 6442450944 | bytes 19922948 | tf_op jit(solution)/shard_map/while/body/eval_jaxpr/qoa,ba->qob/dot_general | solution.py:51
  306.6 0.0 copy-done.2
  306.6 5.7 %select_add_fusion.2 = f32[768,1024]{1,0:T(8,128)S(1)} fusion(f32[768,1024]{1,0:T(8,128)S(1)} %copy-done.2, bf16[12288,1024]{1,0:T(8,128)(2,1)} %get-tuple-element.157, s32[]{:T(128)S(6)} %select_n.144, f32[2,768,2048]{1,2,0:T(8,128)S(1)} %convolution_bitcast_fusion.2, pred[]{:T(512)S(6)} %compare.3), kind=kOutput, calls=%fused_computation.8.clone.1 | convolution fusion | flops 3225944064 | bytes 23068676 | tf_op jit(solution)/shard_map/while/body/eval_jaxpr/dot_general | solution.py:55
  312.3 0.0 copy-start.3
  312.3 1.7 copy-done.3
  314.0 8.7 %convolution_bitcast_fusion.2 = f32[2,768,2048]{1,2,0:T(8,128)S(1)} fusion(bf16[2,768,1024]{2,1,0:T(8,128)(2,1)S(1)} %get-tuple-element.158, bf16[12288,1024]{1,0:T(8,128)(2,1)} %get-tuple-element.157, s32[]{:T(128)S(6)} %select_n.144), kind=kOutput, calls=%fused_computation.2.clone.1 | convolution fusion | flops 6442450944 | bytes 19922948 | tf_op jit(solution)/shard_map/while/body/eval_jaxpr/qoa,ba->qob/dot_general | solution.py:51
  322.8 0.0 copy-done.2
  322.8 5.7 %select_add_fusion.2 = f32[768,1024]{1,0:T(8,128)S(1)} fusion(f32[768,1024]{1,0:T(8,128)S(1)} %copy-done.2, bf16[12288,1024]{1,0:T(8,128)(2,1)} %get-tuple-element.157, s32[]{:T(128)S(6)} %select_n.144, f32[2,768,2048]{1,2,0:T(8,128)S(1)} %convolution_bitcast_fusion.2, pred[]{:T(512)S(6)} %compare.3), kind=kOutput, calls=%fused_computation.8.clone.1 | convolution fusion | flops 3225944064 | bytes 23068676 | tf_op jit(solution)/shard_map/while/body/eval_jaxpr/dot_general | solution.py:55
  328.4 0.0 copy-start.3
  328.4 1.7 copy-done.3
  330.1 6.1 %fusion.22 = f32[1024,1024]{1,0:T(8,128)} fusion(bf16[768,1024]{1,0:T(8,128)(2,1)} %param.8, f32[768,1024]{1,0:T(8,128)} %get-tuple-element.84), kind=kOutput, calls=%fused_computation.24 | convolution fusion | flops 1611399168 | bytes 8912896 | tf_op jit(solution)/shard_map/tsk,sl->ktl/dot_general | solution.py:73
  336.3 0.0 reduce-scatter.3.cloned.1.call-update
  336.3 0.0 reduce-scatter.5.cloned.1.call-start
  336.4 0.0 copy-done
  336.4 0.2 dynamic-slice_reduce_fusion
  336.6 79.8 %reduce-scatter.3.cloned.1.call-done = f32[64,1024]{1,0:T(8,128)} async-done(((f32[1024,1024]{1,0:T(8,128)}), f32[64,1024]{1,0:T(8,128)}) %reduce-scatter.3.cloned.1.call-update) | async-done | bytes 262160 | tf_op jit(solution)/shard_map/reduce_scatter | solution.py:72
  416.4 1.9 multiply_multiply_fusion
  418.2 0.0 reduce-scatter.5.cloned.1.call-update
  418.3 14.0 %reduce-scatter.5.cloned.1.call-done = f32[1,64,1024]{2,1,0:T(8,128)} async-done(((f32[2,64,1024]{2,1,0:T(8,128)}), f32[1,64,1024]{2,1,0:T(8,128)}) %reduce-scatter.5.cloned.1.call-update) | async-done | bytes 262160 | tf_op jit(solution)/shard_map/reduce_scatter | solution.py:81
  (7 shorter events, 0.0 us)
Async XLA Ops:
  6.5 329.8 %copy-start = (f32[2,2]{1,0:T(2,128)S(1)}, f32[2,2]{1,0:T(2,128)}, u32[]{:S(2)}) copy-start(f32[2,2]{1,0:T(2,128)} %param.9) | copy-start | bytes 52
  6.5 226.8 %all-gather.2.cloned.1.call-start = ((), (), s32[]{:S(2)}) async-start(), calls=%async_computation.2 | async-start | bytes 26738688 | tf_op jit(solution)/shard_map/all_gather | solution.py:70
  7.3 409.1 %reduce-scatter.3.cloned.1.call-start = ((), (), s32[]{:S(2)}) async-start(), calls=%async_computation.3 | async-start | bytes 4456448 | tf_op jit(solution)/shard_map/reduce_scatter | solution.py:72
  8.3 1.7 collective-permute-start
  11.2 22.8 %collective-permute-start.1 = (bf16[2,1,128,1024]{3,2,1,0:T(8,128)(2,1)S(1)}, bf16[2,1,128,1024]{3,2,1,0:T(8,128)(2,1)S(1)}, u32[]{:S(2)}, u32[]{:S(2)}) collective-permute-start(bf16[2,1,128,1024]{3,2,1,0:T(8,128)(2,1)S(1)} %fusion.25), channel_id=1, source_target_pairs={{0,2},{1,3},{2,0},{3,1},{4,6},{5,7},{6,4},{7,5},{8,10},{9,11},{10,... | collective-permute-start | bytes 1572872 | tf_op jit(solution)/shard_map/ppermute | solution.py:14
  35.6 47.6 %collective-permute-start.2 = (bf16[2,1,256,1024]{3,2,1,0:T(8,128)(2,1)}, bf16[2,1,256,1024]{3,2,1,0:T(8,128)(2,1)S(1)}, u32[]{:S(2)}, u32[]{:S(2)}) collective-permute-start(bf16[2,1,256,1024]{3,2,1,0:T(8,128)(2,1)} %fusion.24), channel_id=1, source_target_pairs={{0,4},{1,5},{2,6},{3,7},{4,0},{5,1},{6,2},{7,3},{8,12},{9,13},{10,... | collective-permute-start | bytes 3145736 | tf_op jit(solution)/shard_map/ppermute | solution.py:14
  85.8 136.6 %collective-permute-start.3 = (bf16[2,1,512,1024]{3,2,1,0:T(8,128)(2,1)}, bf16[2,1,512,1024]{3,2,1,0:T(8,128)(2,1)}, u32[]{:S(2)}, u32[]{:S(2)}) collective-permute-start(bf16[2,1,512,1024]{3,2,1,0:T(8,128)(2,1)} %fusion.20), channel_id=1, source_target_pairs={{0,8},{1,9},{2,10},{3,11},{4,12},{5,13},{6,14},{7,15},{8,0},{9,1},... | collective-permute-start | bytes 6291464 | tf_op jit(solution)/shard_map/ppermute | solution.py:14
  88.0 134.3 %copy-start.1 = (bf16[768,1024]{1,0:T(8,128)(2,1)S(1)}, bf16[768,1024]{1,0:T(8,128)(2,1)}, u32[]{:S(2)}) copy-start(bf16[768,1024]{1,0:T(8,128)(2,1)} %param.8) | copy-start | bytes 4718596
  233.4 8.7 %copy-start.2 = (f32[768,1024]{1,0:T(8,128)S(1)}, f32[768,1024]{1,0:T(8,128)}, u32[]{:S(2)}) copy-start(f32[768,1024]{1,0:T(8,128)} %get-tuple-element.148) | copy-start | bytes 9437188 | tf_op jit(solution)/shard_map/while
  247.8 1.7 copy-start.3
  249.5 8.7 %copy-start.2 = (f32[768,1024]{1,0:T(8,128)S(1)}, f32[768,1024]{1,0:T(8,128)}, u32[]{:S(2)}) copy-start(f32[768,1024]{1,0:T(8,128)} %get-tuple-element.148) | copy-start | bytes 9437188 | tf_op jit(solution)/shard_map/while
  263.9 1.7 copy-start.3
  265.6 8.7 %copy-start.2 = (f32[768,1024]{1,0:T(8,128)S(1)}, f32[768,1024]{1,0:T(8,128)}, u32[]{:S(2)}) copy-start(f32[768,1024]{1,0:T(8,128)} %get-tuple-element.148) | copy-start | bytes 9437188 | tf_op jit(solution)/shard_map/while
  280.0 1.7 copy-start.3
  281.8 8.7 %copy-start.2 = (f32[768,1024]{1,0:T(8,128)S(1)}, f32[768,1024]{1,0:T(8,128)}, u32[]{:S(2)}) copy-start(f32[768,1024]{1,0:T(8,128)} %get-tuple-element.148) | copy-start | bytes 9437188 | tf_op jit(solution)/shard_map/while
  296.2 1.7 copy-start.3
  297.9 8.7 %copy-start.2 = (f32[768,1024]{1,0:T(8,128)S(1)}, f32[768,1024]{1,0:T(8,128)}, u32[]{:S(2)}) copy-start(f32[768,1024]{1,0:T(8,128)} %get-tuple-element.148) | copy-start | bytes 9437188 | tf_op jit(solution)/shard_map/while
  312.3 1.7 copy-start.3
  314.0 8.7 %copy-start.2 = (f32[768,1024]{1,0:T(8,128)S(1)}, f32[768,1024]{1,0:T(8,128)}, u32[]{:S(2)}) copy-start(f32[768,1024]{1,0:T(8,128)} %get-tuple-element.148) | copy-start | bytes 9437188 | tf_op jit(solution)/shard_map/while
  328.4 1.7 copy-start.3
  336.3 96.0 %reduce-scatter.5.cloned.1.call-start = ((), (), s32[]{:S(2)}) async-start(), calls=%async_computation.4 | async-start | bytes 786432 | tf_op jit(solution)/shard_map/reduce_scatter | solution.py:81
Sparse Core Ops, SparseCore 0:
  8.9 221.4 all-gather.1
  336.4 79.8 reduce-scatter.2
  418.6 13.6 reduce-scatter.4
